TPU v7x, 1024 devices: a whole 8x8x8 slice. The times are simulated.
1024 devices in a mesh: section: 32 (over y, x_hi), row: 2 (over core), col: 16 (over z, x_lo).
Axes of the slice: x: 8 (x_hi: 4, x_lo: 2; x = x_hi * 2 + x_lo), y: 8, z: 8, core: 2. Of those that a mesh axis runs over, the one named last changes fastest.
Arguments:
- inputs: bfloat16 [32, 128, 4096], P('section', 'col', 'row'), may hold values from -6 to 6
- gate_pre: bfloat16 [32, 128, 14336], P('section', None, 'col'), may hold values from -8 to 8
- up_weight: bfloat16 [4096, 14336], P('row', 'col'), may hold values from -0.09375 to 0.09375
- down_weight: bfloat16 [14336, 4096], P('col', 'row'), may hold values from -0.046875 to 0.046875
- output_grad: bfloat16 [32, 128, 4096], P('section', 'col', 'row'), may hold values from -6 to 6
Outputs:
- handed_forward: bfloat16 [32, 128, 4096], P('section', 'col', 'row')
- gate_grad: bfloat16 [32, 128, 14336], P('section', 'row', 'col')
- handed_back: bfloat16 [32, 128, 4096], P('section', 'col', 'row')
All inputs are finite; a program needn't handle non-finite values.
Results may differ from a plain program's by a relative error of at most 0.0041.
Values may be sent and summed in bfloat16 or wider, within the bound.
A program may use at most 32 MiB of HBM per device.

v0:
```python
import jax
import jax.numpy as jnp
from jax import lax
from jax.sharding import PartitionSpec as P


def shifted(value, axis, steps):
    count = lax.axis_size(axis)
    pairs = [(source, (source + steps) % count) for source in range(count)]
    return lax.ppermute(value, axis, pairs)


def row_product(pieces, matrix, contract):
    gathered = lax.all_gather(pieces, "col", axis=0, tiled=True)
    return lax.psum_scatter(
        lax.dot_general(gathered, matrix, (contract, ((), ())), preferred_element_type=jnp.float32),
        "row",
        scatter_dimension=0,
        tiled=True,
    )


def col_product(values, matrix, contract):
    gathered = lax.all_gather(values, "row", axis=0, tiled=True)
    return lax.psum_scatter(
        lax.dot_general(gathered, matrix, (contract, ((), ())), preferred_element_type=jnp.float32),
        "col",
        scatter_dimension=0,
        tiled=True,
    )


def handoff(values, offset):
    return shifted(values, "section", offset)


def shards(inputs, gate_pre, up_weight, down_weight, output_grad):
    activations = inputs[0]
    grad_tile = output_grad[0]
    gate_full = gate_pre[0].astype(jnp.float32)
    own_rows = gate_full.shape[0] // lax.axis_size("row")
    row_start = lax.axis_index("row") * own_rows
    gate_used = lax.dynamic_slice_in_dim(gate_full, row_start, own_rows, 0)
    up_act = row_product(activations, up_weight, ((1,), (0,)))
    sigmoid_gate = jax.nn.sigmoid(gate_used)
    hidden = (gate_used * sigmoid_gate * up_act).astype(jnp.bfloat16)
    mixed = col_product(hidden, down_weight, ((1,), (0,)))
    layer_out = (activations.astype(jnp.float32) + mixed).astype(jnp.bfloat16)
    handed_forward = handoff(layer_out, 1)
    hidden_grad = row_product(grad_tile, down_weight, ((1,), (1,)))
    up_grad = (hidden_grad * gate_used * sigmoid_gate).astype(jnp.bfloat16)
    gate_grad = (
        hidden_grad * up_act * sigmoid_gate * (1.0 + gate_used * (1.0 - sigmoid_gate))
    ).astype(jnp.bfloat16)
    back_sum = col_product(up_grad, up_weight, ((1,), (1,)))
    input_grad = (grad_tile.astype(jnp.float32) + back_sum).astype(jnp.bfloat16)
    handed_back = handoff(input_grad, -1)
    return (handed_forward[None], gate_grad[None], handed_back[None])


def solution(mesh):
    placed = (
        P("section", "col", "row"),
        P("section", None, "col"),
        P("row", "col"),
        P("col", "row"),
        P("section", "col", "row"),
    )
    return jax.shard_map(
        shards,
        mesh=mesh,
        in_specs=placed,
        out_specs=(
            P("section", "col", "row"),
            P("section", "row", "col"),
            P("section", "col", "row"),
        ),
        check_vma=False,
    )
```

profile of v0, /device:TPU:60, one launch (start us, length us, event | category | flops | bytes accessed | tf_op | source)
XLA Modules:
  0.0 301.4 jit_solution(10728974125305859342)
XLA Ops:
  7.2 0.0 copy-start.1
  7.2 0.0 reduce-scatter.5.cloned.1.call-start
  7.2 49.9 %all-gather = bf16[1,128,2048]{2,1,0:T(8,128)(2,1)S(1)} all-gather(bf16[1,8,2048]{2,1,0:T(8,128)(2,1)} %param.5), channel_id=2, replica_groups=mesh['section'=32,'row'=2,'col'=16] {'col'}, dimensions={1}, use_global_device_ids=true | all-gather | bytes 557056 | tf_op jit(solution)/shard_map/all_gather | solution.py:14
  57.1 3.5 %fusion.2 = f32[128,896]{1,0:T(8,128)} fusion(bf16[2048,896]{1,0:T(8,128)(2,1)} %param.7, bf16[1,128,2048]{2,1,0:T(8,128)(2,1)S(1)} %all-gather), kind=kOutput, calls=%fused_computation.2 | convolution fusion | flops 469762048 | bytes 4653056 | tf_op jit(solution)/shard_map/dot_general | solution.py:16
  60.6 0.0 copy-start.2
  60.6 0.0 reduce-scatter.5.cloned.1.call-update
  60.7 0.0 reduce-scatter.9.cloned.1.call-start
  60.7 0.0 copy-done.1
  60.7 34.0 %all-gather.1 = bf16[1,128,2048]{2,1,0:T(8,128)(2,1)S(1)} all-gather(bf16[1,8,2048]{2,1,0:T(8,128)(2,1)S(1)} %copy-done.1), channel_id=3, replica_groups=mesh['section'=32,'row'=2,'col'=16] {'col'}, dimensions={1}, use_global_device_ids=true | all-gather | bytes 557056 | tf_op jit(solution)/shard_map/all_gather | solution.py:14
  94.8 4.1 %fusion = f32[128,896]{1,0:T(8,128)} fusion(bf16[896,2048]{1,0:T(8,128)(2,1)} %param.8, bf16[1,128,2048]{2,1,0:T(8,128)(2,1)S(1)} %all-gather.1), kind=kOutput, calls=%fused_computation | convolution fusion | flops 469762048 | bytes 4653056 | tf_op jit(solution)/shard_map/dot_general | solution.py:16
  98.8 0.0 reduce-scatter.9.cloned.1.call-update
  98.9 0.0 reduce-scatter.7.cloned.1.call-start
  98.9 0.0 reduce-scatter.5.cloned.1.call-done
  99.0 15.2 %reduce-scatter.9.cloned.1.call-done = f32[64,896]{1,0:T(8,128)} async-done(((f32[128,896]{1,0:T(8,128)}), f32[64,896]{1,0:T(8,128)}) %reduce-scatter.9.cloned.1.call-update) | async-done | bytes 229392 | tf_op jit(solution)/shard_map/reduce_scatter | solution.py:15
  114.1 0.0 copy-done.2
  114.1 1.8 fusion.13
  116.0 2.0 all_gather.13
  117.9 3.7 %fusion.17 = f32[128,2048]{1,0:T(8,128)} fusion(bf16[128,896]{1,0:T(8,128)(2,1)S(1)} %all_gather.13, bf16[896,2048]{1,0:T(8,128)(2,1)} %param.8), kind=kOutput, calls=%fused_computation.23 | convolution fusion | flops 469762048 | bytes 4947968 | tf_op jit(solution)/shard_map/dot_general | solution.py:26
  121.6 0.0 copy-start
  121.6 0.0 reduce-scatter.7.cloned.1.call-update
  121.7 0.0 reduce-scatter.11.cloned.1.call-start
  121.7 2.0 all_gather.15
  123.7 4.4 %fusion.18 = f32[128,2048]{1,0:T(8,128)} fusion(bf16[128,896]{1,0:T(8,128)(2,1)S(1)} %all_gather.15, bf16[2048,896]{1,0:T(8,128)(2,1)} %param.7), kind=kOutput, calls=%fused_computation.24 | convolution fusion | flops 469762048 | bytes 4947968 | tf_op jit(solution)/shard_map/dot_general | solution.py:26
  128.0 0.0 reduce-scatter.11.cloned.1.call-update
  128.1 74.8 %reduce-scatter.7.cloned.1.call-done = f32[8,2048]{1,0:T(8,128)} async-done(((f32[128,2048]{1,0:T(8,128)}), f32[8,2048]{1,0:T(8,128)}) %reduce-scatter.7.cloned.1.call-update) | async-done | bytes 65552 | tf_op jit(solution)/shard_map/reduce_scatter | solution.py:25
  202.9 0.0 copy-done
  202.9 0.8 fusion.16
  203.7 5.8 %collective-permute-start = (bf16[8,2048]{1,0:T(8,128)(2,1)S(1)}, bf16[8,2048]{1,0:T(8,128)(2,1)S(1)}, u32[]{:S(2)}, u32[]{:S(2)}) collective-permute-start(bf16[8,2048]{1,0:T(8,128)(2,1)S(1)} %fusion.16), channel_id=1, source_target_pairs={{0,32},{32,64},{64,96},{96,128},{128,160},{160,192},{192,224},{224... | collective-permute-start | bytes 98312 | tf_op jit(solution)/shard_map/ppermute | solution.py:10
  209.5 73.3 %reduce-scatter.11.cloned.1.call-done = f32[8,2048]{1,0:T(8,128)} async-done(((f32[128,2048]{1,0:T(8,128)}), f32[8,2048]{1,0:T(8,128)}) %reduce-scatter.11.cloned.1.call-update) | async-done | bytes 65552 | tf_op jit(solution)/shard_map/reduce_scatter | solution.py:25
  282.7 0.8 fusion.15
  283.6 4.4 %collective-permute-start.1 = (bf16[8,2048]{1,0:T(8,128)(2,1)S(1)}, bf16[8,2048]{1,0:T(8,128)(2,1)S(1)}, u32[]{:S(2)}, u32[]{:S(2)}) collective-permute-start(bf16[8,2048]{1,0:T(8,128)(2,1)S(1)} %fusion.15), channel_id=1, source_target_pairs={{0,992},{32,0},{64,32},{96,64},{128,96},{160,128},{192,160},{224,1... | collective-permute-start | bytes 98312 | tf_op jit(solution)/shard_map/ppermute | solution.py:10
  288.0 0.0 collective-permute-done
  288.0 5.6 %collective-permute-done.1 = bf16[8,2048]{1,0:T(8,128)(2,1)S(1)} collective-permute-done((bf16[8,2048]{1,0:T(8,128)(2,1)S(1)}, bf16[8,2048]{1,0:T(8,128)(2,1)S(1)}, u32[]{:S(2)}, u32[]{:S(2)}) %collective-permute-start.1) | collective-permute-done | bytes 32800 | tf_op jit(solution)/shard_map/ppermute | solution.py:10
  293.6 0.6 copy.10
  294.2 0.6 copy.11
Async XLA Ops:
  7.2 53.6 %copy-start.1 = (bf16[1,8,2048]{2,1,0:T(8,128)(2,1)S(1)}, bf16[1,8,2048]{2,1,0:T(8,128)(2,1)}, u32[]{:S(2)}) copy-start(bf16[1,8,2048]{2,1,0:T(8,128)(2,1)} %param.9) | copy-start | bytes 98308
  7.2 91.8 %reduce-scatter.5.cloned.1.call-start = ((), (), s32[]{:S(2)}) async-start(), calls=%async_computation.4 | async-start | bytes 688128 | tf_op jit(solution)/shard_map/reduce_scatter | solution.py:15
  60.6 53.5 %copy-start.2 = (bf16[1,128,896]{2,1,0:T(8,128)(2,1)S(1)}, bf16[1,128,896]{2,1,0:T(8,128)(2,1)}, u32[]{:S(2)}) copy-start(bf16[1,128,896]{2,1,0:T(8,128)(2,1)} %param.6) | copy-start | bytes 688132
  60.7 53.5 %reduce-scatter.9.cloned.1.call-start = ((), (), s32[]{:S(2)}) async-start(), calls=%async_computation.6 | async-start | bytes 688128 | tf_op jit(solution)/shard_map/reduce_scatter | solution.py:15
  98.9 104.0 %reduce-scatter.7.cloned.1.call-start = ((), (), s32[]{:S(2)}) async-start(), calls=%async_computation.5 | async-start | bytes 1114112 | tf_op jit(solution)/shard_map/reduce_scatter | solution.py:25
  121.6 81.2 %copy-start = (bf16[1,8,2048]{2,1,0:T(8,128)(2,1)S(1)}, bf16[1,8,2048]{2,1,0:T(8,128)(2,1)}, u32[]{:S(2)}) copy-start(bf16[1,8,2048]{2,1,0:T(8,128)(2,1)} %param.5) | copy-start | bytes 98308
  121.7 161.1 %reduce-scatter.11.cloned.1.call-start = ((), (), s32[]{:S(2)}) async-start(), calls=%async_computation.7 | async-start | bytes 1114112 | tf_op jit(solution)/shard_map/reduce_scatter | solution.py:25
  203.7 84.3 %collective-permute-start = (bf16[8,2048]{1,0:T(8,128)(2,1)S(1)}, bf16[8,2048]{1,0:T(8,128)(2,1)S(1)}, u32[]{:S(2)}, u32[]{:S(2)}) collective-permute-start(bf16[8,2048]{1,0:T(8,128)(2,1)S(1)} %fusion.16), channel_id=1, source_target_pairs={{0,32},{32,64},{64,96},{96,128},{128,160},{160,192},{192,224},{224... | collective-permute-start | bytes 98312 | tf_op jit(solution)/shard_map/ppermute | solution.py:10
  283.6 10.0 %collective-permute-start.1 = (bf16[8,2048]{1,0:T(8,128)(2,1)S(1)}, bf16[8,2048]{1,0:T(8,128)(2,1)S(1)}, u32[]{:S(2)}, u32[]{:S(2)}) collective-permute-start(bf16[8,2048]{1,0:T(8,128)(2,1)S(1)} %fusion.15), channel_id=1, source_target_pairs={{0,992},{32,0},{64,32},{96,64},{128,96},{160,128},{192,160},{224,1... | collective-permute-start | bytes 98312 | tf_op jit(solution)/shard_map/ppermute | solution.py:10
Sparse Core Ops, SparseCore 0:
  60.8 14.3 reduce-scatter.4
  99.0 15.0 reduce-scatter.8
  121.8 81.0 reduce-scatter.6
  206.5 76.2 reduce-scatter.10
where the time goes:
time: 302 us; the launch traced here: 301 us
  waiting for transfers between devices  169 us (56%)
  blocking collectives  87.8 us (29%)
  matrix products  15.7 us (5%)
  between operations  13.8 us (5%)
  starting transfers between devices  10.3 us (3%)
  other arithmetic  3.52 us (1%)
    reduce_scatter x2, waiting for transfers between devices, col_product(): lax.psum_scatter(lax.dot_general(gathered, matrix, (contract, ((), ())),...  148 us
    all_gather x2, blocking collectives, row_product(): gathered = lax.all_gather(pieces, 'col', axis=0, tiled=True)  83.9 us
    reduce_scatter x2, waiting for transfers between devices, row_product(): lax.psum_scatter(lax.dot_general(gathered, matrix, (contract, ((), ())),...  15.2 us
    ppermute x2, starting transfers between devices, shifted(): return lax.ppermute(value, axis, pairs)  10.2 us
    dot_general x2, matrix products, col_product(): lax.dot_general(gathered, matrix, (contract, ((), ())), preferred_element...  8.09 us
    dot_general x2, matrix products, row_product(): lax.dot_general(gathered, matrix, (contract, ((), ())), preferred_element...  7.64 us
  transfers between devices with their start and end apart: 6, of which 4 were waited for; matrix products, arithmetic and copies ran while one was open for 3% of the time, Pallas kernels for 0%

commit v1 on v0

v1 whole, which is shorter than its diff:
```python
import functools

import jax
import jax.numpy as jnp
from jax import lax
from jax.experimental import pallas as pl
from jax.experimental.pallas import tpu as pltpu
from jax.sharding import PartitionSpec as P

MESH = pl.DeviceIdType.MESH
F32 = jnp.float32
BF16 = jnp.bfloat16
NT = (((1,), (1,)), ((), ()))
NN = (((1,), (0,)), ((), ()))


def kernel(
    in_f, gate_in, up_in, dn_in, in_b,
    out_f, out_g, out_b,
    gf, gb, upv, dnv, gv, gs, dg,
    uf, hb, s1f, r1f, s1b, r1b, gg,
    pf, pb, sxf, rxf, sfp, rfp, sfm, rfm, sbp, rbp, sbm, rbm, sxb, rxb, hf, hbk,
    lsem, fzp_s, fzp_r, fzm_s, fzm_r, fx_s, fx_r, bzp_s, bzp_r, bzm_s, bzm_r, bx_s, bx_r,
    e_s, e_r, ffx_s, ffx_r, rfp_s, rfp_r, rfm_s, rfm_r, rbp_s, rbp_r, rbm_s, rbm_r, rx_s, rx_r, ho_s, ho_r,
):
    s = lax.axis_index("section")
    r = lax.axis_index("row")
    c = lax.axis_index("col")
    z, xl = c // 2, c % 2
    xo = 1 - xl
    ns = lax.axis_size("section")
    zp = {"col": ((z + 1) % 8) * 2 + xl}
    zm = {"col": ((z + 7) % 8) * 2 + xl}
    xp = {"col": z * 2 + xo}
    mate = {"row": 1 - r}
    nxt = {"section": (s + 1) % ns}
    prv = {"section": (s + ns - 1) % ns}

    local = []

    def fetch(src, dst, i):
        cp = pltpu.make_async_copy(src, dst, lsem.at[i])
        cp.start()
        return cp

    cp_gate = fetch(gate_in.at[0], gv, 0)
    cp_f = fetch(in_f.at[0], gf.at[z, xl], 1)
    cp_b = fetch(in_b.at[0], gb.at[z, xl], 2)
    cp_up = fetch(up_in, upv, 3)
    cp_dn = fetch(dn_in, dnv, 4)

    barrier = pltpu.get_barrier_semaphore()
    for dev in (zp, zm, xp, mate, nxt, prv):
        pl.semaphore_signal(barrier, inc=1, device_id=dev, device_id_type=MESH)
    pl.semaphore_wait(barrier, 6)

    sent = []

    def put(src, dst, ss, rs, dev):
        cp = pltpu.make_async_remote_copy(
            src_ref=src, dst_ref=dst, send_sem=ss, recv_sem=rs, device_id=dev, device_id_type=MESH
        )
        cp.start()
        sent.append(cp)

    def got(dst, rs):
        pltpu.make_async_remote_copy(
            src_ref=dst, dst_ref=dst, send_sem=rs, recv_sem=rs, device_id=zp, device_id_type=MESH
        ).wait_recv()

    put(in_f.at[0], gf.at[z, xl], fzp_s.at[0], fzp_r.at[0], zp)
    put(in_f.at[0], gf.at[z, xl], fzm_s.at[0], fzm_r.at[0], zm)
    put(in_b.at[0], gb.at[z, xl], bx_s.at[0], bx_r.at[0], xp)
    put(in_b.at[0], gb.at[z, xl], bzp_s.at[0], bzp_r.at[0], zp)
    put(in_b.at[0], gb.at[z, xl], bzm_s.at[0], bzm_r.at[0], zm)
    put(in_f.at[0], gf.at[z, xl], fx_s.at[0], fx_r.at[0], xp)

    cp_gate.wait()
    g32 = gv[...].astype(F32)
    sg = 1.0 / (1.0 + jnp.exp(-g32))
    gs[...] = g32 * sg
    dg[...] = sg * (1.0 + g32 * (1.0 - sg))

    for d in range(1, 5):
        lo, hi = (z + 8 - d) % 8, (z + d) % 8
        got(gf.at[lo, xl], fzp_r.at[d - 1])
        if d < 4:
            put(gf.at[lo, xl], gf.at[lo, xl], fzp_s.at[d], fzp_r.at[d], zp)
        put(gf.at[lo, xl], gf.at[lo, xl], fx_s.at[d], fx_r.at[d], xp)
        if d <= 3:
            got(gf.at[hi, xl], fzm_r.at[d - 1])
            if d < 3:
                put(gf.at[hi, xl], gf.at[hi, xl], fzm_s.at[d], fzm_r.at[d], zm)
            put(gf.at[hi, xl], gf.at[hi, xl], fx_s.at[4 + d], fx_r.at[4 + d], xp)
        if d == 1:
            got(gb.at[z, xo], bx_r.at[0])
            put(gb.at[z, xo], gb.at[z, xo], bzp_s.at[3], bzp_r.at[3], zp)
            put(gb.at[z, xo], gb.at[z, xo], bzm_s.at[4], bzm_r.at[4], zm)
        for half, x in ((0, xl), (1, xo)):
            if d <= 3:
                i = half * 3 + d - 1
                got(gb.at[lo, x], bzp_r.at[i])
                if d < 3:
                    put(gb.at[lo, x], gb.at[lo, x], bzp_s.at[i + 1], bzp_r.at[i + 1], zp)
            i = half * 4 + d - 1
            got(gb.at[hi, x], bzm_r.at[i])
            if d < 4:
                put(gb.at[hi, x], gb.at[hi, x], bzm_s.at[i + 1], bzm_r.at[i + 1], zm)
    got(gf.at[z, xo], fx_r.at[0])
    for d in range(1, 5):
        got(gf.at[(z + 8 - d) % 8, xo], fx_r.at[d])
        if d <= 3:
            got(gf.at[(z + d) % 8, xo], fx_r.at[4 + d])
    cp_f.wait()
    cp_b.wait()
    cp_up.wait()
    cp_dn.wait()

    cuts = ((0, 512), (512, 384))
    act = gf[...].reshape(128, 2048)
    for i, (a, w) in enumerate(cuts):
        v = lax.dot_general(act, upv[:, a : a + w], NN, preferred_element_type=F32)
        uf[:, a : a + w] = v
        s1f[:, a : a + w] = v.astype(BF16)
        put(s1f.at[:, a : a + w], r1f.at[:, a : a + w], e_s.at[i], e_r.at[i], mate)
    grd = gb[...].reshape(128, 2048)
    for i, (a, w) in enumerate(cuts):
        v = lax.dot_general(grd, dnv[a : a + w, :], NT, preferred_element_type=F32)
        hb[:, a : a + w] = v
        s1b[:, a : a + w] = v.astype(BF16)
        put(s1b.at[:, a : a + w], r1b.at[:, a : a + w], e_s.at[2 + i], e_r.at[2 + i], mate)

    for i, (a, w) in enumerate(cuts):
        got(r1f.at[:, a : a + w], e_r.at[i])
    u = uf[...] + r1f[...].astype(F32)
    uf[...] = u
    hid = (gs[...] * u).astype(BF16)
    for a in range(0, 2048, 512):
        v = lax.dot_general(hid, dnv[:, a : a + 512], NN, preferred_element_type=F32)
        pf[:, :, :, a : a + 512] = v.reshape(8, 2, 8, 512)
    order = (4, 3, -3, 2, -2, 1, -1, 0)
    for i, d in enumerate(order):
        sxf[i] = pf[(z + d + 8) % 8, xo].astype(BF16)
        put(sxf.at[i], rxf.at[i], ffx_s.at[i], ffx_r.at[i], xp)

    for i, (a, w) in enumerate(cuts):
        got(r1b.at[:, a : a + w], e_r.at[2 + i])
    h = hb[...] + r1b[...].astype(F32)
    hb[...] = h
    upg = (gs[...] * h).astype(BF16)
    for a in range(0, 2048, 512):
        v = lax.dot_general(upg, upv[a : a + 512, :], NT, preferred_element_type=F32)
        pb[:, :, :, a : a + 512] = v.reshape(8, 2, 8, 512)

    def own_f(d):
        i = order.index(d)
        got(rxf.at[i], ffx_r.at[i])
        return pf[(z + d + 8) % 8, xl] + rxf[i].astype(F32)

    for k in range(4):
        if k == 0:
            sbm[0] = pb[(z + 4) % 8].astype(BF16)
            put(sbm.at[0], rbm.at[0], rbm_s.at[0], rbm_r.at[0], zm)
            sbp[0] = pb[(z + 3) % 8].astype(BF16)
            put(sbp.at[0], rbp.at[0], rbp_s.at[0], rbp_r.at[0], zp)
            sfp[0] = own_f(4).astype(BF16)
            put(sfp.at[0], rfp.at[0], rfp_s.at[0], rfp_r.at[0], zp)
            sfm[0] = own_f(-3).astype(BF16)
            put(sfm.at[0], rfm.at[0], rfm_s.at[0], rfm_r.at[0], zm)
            rows = pl.ds(pl.multiple_of(r * 64, 64), 64)
            gg[...] = (hb[rows, :] * uf[rows, :] * dg[rows, :]).astype(BF16)
            cp_g = fetch(gg, out_g.at[0], 0)
        else:
            got(rbm.at[k - 1], rbm_r.at[k - 1])
            sbm[k] = (pb[(z + 4 + k) % 8] + rbm[k - 1].astype(F32)).astype(BF16)
            put(sbm.at[k], rbm.at[k], rbm_s.at[k], rbm_r.at[k], zm)
            if k < 3:
                got(rbp.at[k - 1], rbp_r.at[k - 1])
                sbp[k] = (pb[(z + 3 - k) % 8] + rbp[k - 1].astype(F32)).astype(BF16)
                put(sbp.at[k], rbp.at[k], rbp_s.at[k], rbp_r.at[k], zp)
            v = own_f(4 - k)
            got(rfp.at[k - 1], rfp_r.at[k - 1])
            sfp[k] = (v + rfp[k - 1].astype(F32)).astype(BF16)
            put(sfp.at[k], rfp.at[k], rfp_s.at[k], rfp_r.at[k], zp)
            if k < 3:
                v = own_f(k - 3)
                got(rfm.at[k - 1], rfm_r.at[k - 1])
                sfm[k] = (v + rfm[k - 1].astype(F32)).astype(BF16)
                put(sfm.at[k], rfm.at[k], rfm_s.at[k], rfm_r.at[k], zm)

    got(rbp.at[2], rbp_r.at[2])
    got(rbm.at[3], rbm_r.at[3])
    sxb[...] = (pb[z, xo] + rbp[2, xo].astype(F32) + rbm[3, xo].astype(F32)).astype(BF16)
    put(sxb, rxb, rx_s.at[0], rx_r.at[0], xp)

    v = own_f(0) + gf[z, xl].astype(F32)
    got(rfm.at[2], rfm_r.at[2])
    got(rfp.at[3], rfp_r.at[3])
    hf[...] = (v + rfm[2].astype(F32) + rfp[3].astype(F32)).astype(BF16)
    put(hf, out_f.at[0], ho_s.at[0], ho_r.at[0], nxt)

    v = pb[z, xl] + rbp[2, xl].astype(F32) + rbm[3, xl].astype(F32) + gb[z, xl].astype(F32)
    got(rxb, rx_r.at[0])
    hbk[...] = (v + rxb[...].astype(F32)).astype(BF16)
    put(hbk, out_b.at[0], ho_s.at[1], ho_r.at[1], prv)

    cp_g.wait()
    for cp in sent:
        cp.wait_send()
    got(out_f.at[0], ho_r.at[0])
    got(out_b.at[0], ho_r.at[1])


def shards(inputs, gate_pre, up_weight, down_weight, output_grad):
    vm = pltpu.VMEM
    dma = lambda n: [pltpu.SemaphoreType.DMA((n,)), pltpu.SemaphoreType.DMA((n,))]
    blk = lambda *n: vm((*n, 8, 2048), BF16)
    mat = lambda t: vm((128, 896), t)
    any_spec = pl.BlockSpec(memory_space=pl.ANY)
    return pl.pallas_call(
        kernel,
        out_shape=(
            jax.ShapeDtypeStruct((1, 8, 2048), BF16),
            jax.ShapeDtypeStruct((1, 64, 896), BF16),
            jax.ShapeDtypeStruct((1, 8, 2048), BF16),
        ),
        in_specs=[any_spec] * 5,
        out_specs=(any_spec,) * 3,
        scratch_shapes=[
            blk(8, 2), blk(8, 2), vm((2048, 896), BF16), vm((896, 2048), BF16), mat(BF16), mat(F32), mat(F32),
            mat(F32), mat(F32), mat(BF16), mat(BF16), mat(BF16), mat(BF16), vm((64, 896), BF16),
            vm((8, 2, 8, 2048), F32), vm((8, 2, 8, 2048), F32),
            blk(8), blk(8), blk(4), blk(4), blk(3), blk(3), blk(3, 2), blk(3, 2), blk(4, 2), blk(4, 2),
            blk(), blk(), blk(), blk(),
            pltpu.SemaphoreType.DMA((5,)),
            *dma(4), *dma(3), *dma(8), *dma(6), *dma(8), *dma(1),
            *dma(4), *dma(8), *dma(4), *dma(3), *dma(3), *dma(4), *dma(1), *dma(2),
        ],
        compiler_params=pltpu.CompilerParams(
            collective_id=0, has_side_effects=True, vmem_limit_bytes=60 * 1024 * 1024
        ),
        name="ffn",
    )(inputs, gate_pre, up_weight, down_weight, output_grad)


def solution(mesh):
    placed = (
        P("section", "col", "row"),
        P("section", None, "col"),
        P("row", "col"),
        P("col", "row"),
        P("section", "col", "row"),
    )
    return jax.shard_map(
        shards,
        mesh=mesh,
        in_specs=placed,
        out_specs=(
            P("section", "col", "row"),
            P("section", "row", "col"),
            P("section", "col", "row"),
        ),
        check_vma=False,
    )
```

time: 302 us -> 69.1 us (0.23)
  the two profiles are of different devices: /device:TPU:60 before, /device:TPU:126 now
where the time goes in v1:
time: 69.1 us; the launch traced here: 68.8 us
  Pallas kernels  63.9 us (92%)
  local copies, waits for them, and re-layouts  4.3 us (6%)
    pallas_call x1, Pallas kernels, shards(): pl.pallas_call(kernel, out_shape=(jax.ShapeDtypeStruct((1, 8, 2048), BF16...  63.9 us
    unnamed x3, local copies, waits for them, and re-layouts  4.3 us

profile of v1, /device:TPU:126, one launch (start us, length us, event | category | flops | bytes accessed | tf_op | source)
XLA Modules:
  0.0 68.8 jit_solution(6259121652497225035)
XLA Ops:
  0.6 63.9 %ffn.1 = (bf16[1,8,2048]{2,1,0:T(8,128)(2,1)}, bf16[1,64,896]{2,1,0:T(8,128)(2,1)}, bf16[1,8,2048]{2,1,0:T(8,128)(2,1)}) custom-call(bf16[1,8,2048]{2,1,0:T(8,128)(2,1)} %in_f.1, bf16[1,128,896]{2,1,0:T(8,128)(2,1)} %gate_in.1, bf16[2048,896]{1,0:T(8,128)(2,1)} %up_in.1, bf16[896,2048]{1,0:T(8,128)(2,1)} %dn_in.1, bf16[1,8,2048]{2,1,0:T(8,128)(2,1)} %in_b.1), custom_call_target="tpu_custom_call" | custom-call | tf_op jit(solution)/shard_map/ffn/pallas_call | solution.py:220
  64.5 1.4 %copy.11 = bf16[1,8,2048]{2,1,0:T(8,128)(2,1)} copy(bf16[1,8,2048]{2,1,0:T(8,128)(2,1)} %get-tuple-element.6) | data formatting | bytes 65536
  65.9 1.6 %copy.12 = bf16[1,64,896]{2,1,0:T(8,128)(2,1)} copy(bf16[1,64,896]{2,1,0:T(8,128)(2,1)} %get-tuple-element.7) | data formatting | bytes 229376
  67.5 1.4 %copy.13 = bf16[1,8,2048]{2,1,0:T(8,128)(2,1)} copy(bf16[1,8,2048]{2,1,0:T(8,128)(2,1)} %get-tuple-element.8) | data formatting | bytes 65536

commit v2 on v0

v2 whole, which is shorter than its diff:
```python
import jax
import jax.numpy as jnp
from jax import lax
from jax.experimental import pallas as pl
from jax.experimental.pallas import tpu as pltpu
from jax.sharding import PartitionSpec as P

MESH = pl.DeviceIdType.MESH
F32 = jnp.float32
BF16 = jnp.bfloat16
NT = (((1,), (1,)), ((), ()))
NN = (((1,), (0,)), ((), ()))
CUTS = ((0, 512), (512, 384))
B_LEN = (4, 3)
F_LEN = (3, 4)


def kernel(
    in_f, gate_in, up_in, dn_in, in_b,
    out_f, out_g, out_b,
    gf, gb, upv, dnv, gv, gs, dg,
    uf, hb, s1f, r1f, s1b, r1b, gg,
    pf, pb, sfp, rfp, sfm, rfm, sbp, rbp, sbm, rbm, sxf, rxf, sxb, rxb,
    m1f, n1f, m1b, n1b, mf, mb, of, ob,
    lsem, near, far, afp_s, afp_r, afm_s, afm_r, abp_s, abp_r, abm_s, abm_r, ax_s, ax_r,
    e_s, e_r, rfp_s, rfp_r, rfm_s, rfm_r, rbp_s, rbp_r, rbm_s, rbm_r, rx_s, rx_r,
    h1_s, h1_r, hf_s, hf_r, hb_s, hb_r,
):
    s = lax.axis_index("section")
    r = lax.axis_index("row")
    c = lax.axis_index("col")
    z, xl = c // 2, c % 2
    xo = 1 - xl
    ns = lax.axis_size("section")
    sp, sm = (s + 1) % ns, (s + ns - 1) % ns
    up1, dn1 = (z + 1) % 8, (z + 7) % 8
    zp = {"col": up1 * 2 + xl}
    zm = {"col": dn1 * 2 + xl}
    xp = {"col": z * 2 + xo}
    mate = {"row": 1 - r}

    def at(sec, zz, x):
        return {"section": sec, "col": zz * 2 + x}

    def fetch(src, dst, i):
        cp = pltpu.make_async_copy(src, dst, lsem.at[i])
        cp.start()
        return cp

    cp_gate = fetch(gate_in.at[0], gv, 0)
    cp_f = fetch(in_f.at[0], gf.at[z, xl], 1)
    cp_b = fetch(in_b.at[0], gb.at[z, xl], 2)
    cp_dn = fetch(dn_in, dnv, 4)
    cp_up = fetch(up_in, upv, 3)

    barrier = pltpu.get_barrier_semaphore()
    greet = [xp, mate, zm]
    for sec in (sp, sm):
        greet += [at(sec, z, xl), at(sec, dn1, xl), at(sec, dn1, xo)]
    for dev in greet:
        pl.semaphore_signal(barrier, inc=1, device_id=dev, device_id_type=MESH)
    pl.semaphore_wait(barrier, 9)

    sent = []

    def rc(src, dst, ss, rs, dev):
        return pltpu.make_async_remote_copy(
            src_ref=src, dst_ref=dst, send_sem=ss, recv_sem=rs, device_id=dev, device_id_type=MESH
        )

    def put(src, dst, ss, rs, dev, keep=True):
        cp = rc(src, dst, ss, rs, dev)
        cp.start()
        if keep:
            sent.append(cp)

    def got(dst, rs):
        rc(dst, dst, rs, rs, zp).wait_recv()

    pl.semaphore_signal(near, inc=1, device_id=zp, device_id_type=MESH)
    put(in_b.at[0], gb.at[z, xl], ax_s.at[0], ax_r.at[0], xp)
    put(in_f.at[0], gf.at[z, xl], ax_s.at[1], ax_r.at[1], xp)
    for sec in (sp, sm):
        for x in (xl, xo):
            pl.semaphore_signal(far, inc=1, device_id=at(sec, up1, x), device_id_type=MESH)

    plus = {0: (gb, abp_s, abp_r, B_LEN[0]), 1: (gf, afp_s, afp_r, F_LEN[0])}
    minus = {0: (gb, abm_s, abm_r, B_LEN[1]), 1: (gf, afm_s, afm_r, F_LEN[1])}

    def send_plus(t, d, o):
        buf, ss, rs, _ = plus[t]
        put(buf.at[o], buf.at[o], ss.at[d], rs.at[d], zp, False)

    def send_minus(t, d, o):
        buf, ss, rs, _ = minus[t]
        put(buf.at[o], buf.at[o], ss.at[d], rs.at[d], zm, False)

    def recv_plus(t, keep):
        buf, ss, rs, n = plus[t]
        for d in range(1, n + 1):
            def step(d=d):
                o = (z + 8 - d) % 8
                got(buf.at[o], rs.at[d - 1])
                if d < n:
                    send_plus(t, d, o)
            pl.when(keep(d))(step)

    def recv_minus(t, keep):
        buf, ss, rs, n = minus[t]
        for d in range(1, n + 1):
            def step(d=d):
                o = (z + d) % 8
                got(buf.at[o], rs.at[d - 1])
                if d < n:
                    send_minus(t, d, o)
            pl.when(keep(d))(step)

    cp_b.wait()
    got(gb.at[z, xo], ax_r.at[0])
    send_plus(0, 0, z)
    cp_f.wait()
    got(gf.at[z, xo], ax_r.at[1])

    @pl.when(z > 0)
    def _():
        pl.semaphore_wait(near, 1)
        send_minus(0, 0, z)
        send_minus(1, 0, z)

    cp_gate.wait()
    g32 = gv[...].astype(F32)
    sg = 1.0 / (1.0 + jnp.exp(-g32))
    gs[...] = g32 * sg
    dg[...] = sg * (1.0 + g32 * (1.0 - sg))

    recv_plus(0, lambda d: d <= z)
    send_plus(1, 0, z)
    recv_plus(1, lambda d: (d <= z) & (z < 7))

    @pl.when(z == 0)
    def _():
        pl.semaphore_wait(near, 1)
        send_minus(0, 0, z)

    recv_minus(0, lambda d: d <= 7 - z)

    @pl.when(z == 0)
    def _():
        send_minus(1, 0, z)

    recv_minus(1, lambda d: d <= 7 - z)
    recv_plus(0, lambda d: d > z)
    recv_minus(0, lambda d: d > 7 - z)

    cp_dn.wait()
    grd = gb[...].reshape(128, 2048)
    for i, (a, w) in enumerate(CUTS):
        v = lax.dot_general(grd, dnv[a : a + w, :], NT, preferred_element_type=F32)
        hb[:, a : a + w] = v
        s1b[:, a : a + w] = v.astype(BF16)
        put(s1b.at[:, a : a + w], r1b.at[:, a : a + w], e_s.at[2 + i], e_r.at[2 + i], mate)

    recv_plus(1, lambda d: (d > z) | (z == 7))
    recv_minus(1, lambda d: d > 7 - z)

    cp_up.wait()
    act = gf[...].reshape(128, 2048)
    for i, (a, w) in enumerate(CUTS):
        v = lax.dot_general(act, upv[:, a : a + w], NN, preferred_element_type=F32)
        uf[:, a : a + w] = v
        s1f[:, a : a + w] = v.astype(BF16)
        put(s1f.at[:, a : a + w], r1f.at[:, a : a + w], e_s.at[i], e_r.at[i], mate)

    chains = {
        (0, 0): (pb, sbp, rbp, rbp_s, rbp_r, B_LEN[0]),
        (0, 1): (pb, sbm, rbm, rbm_s, rbm_r, B_LEN[1]),
        (1, 0): (pf, sfp, rfp, rfp_s, rfp_r, F_LEN[0]),
        (1, 1): (pf, sfm, rfm, rfm_s, rfm_r, F_LEN[1]),
    }
    ends = {0: (mb, hb_s, hb_r, sm), 1: (mf, hf_s, hf_r, sp)}

    def chain(t, way, k):
        part, snd, rcv, ss, rs, n = chains[t, way]
        if k >= n:
            return
        d = n - k
        target = (z + d) % 8 if way == 0 else (z + 8 - d) % 8
        v = part[target]
        if k > 0:
            got(rcv.at[k - 1], rs.at[k - 1])
            v = v + rcv[k - 1].astype(F32)
        snd[k] = v.astype(BF16)
        if d > 1:
            put(snd.at[k], rcv.at[k], ss.at[k], rs.at[k], zp if way == 0 else zm)
        else:
            land, fs, fr, sec = ends[t]
            for j, x in enumerate((xl, xo)):
                i = way * 2 + j
                put(snd.at[k, x], land.at[i], fs.at[i], fr.at[i], at(sec, target, x))

    def share(t, part, snd, rcv):
        snd[...] = part[z, xo].astype(BF16)
        put(snd, rcv, rx_s.at[t], rx_r.at[t], xp)

    def hand(t, part, rcv, buf, m, n, sec):
        got(rcv, rx_r.at[t])
        m[...] = part[z, xl] + buf[z, xl].astype(F32) + rcv[...].astype(F32)
        put(m, n, h1_s.at[t], h1_r.at[t], at(sec, z, xl))

    for i, (a, w) in enumerate(CUTS):
        got(r1b.at[:, a : a + w], e_r.at[2 + i])
    h = hb[...] + r1b[...].astype(F32)
    hb[...] = h
    upg = (gs[...] * h).astype(BF16)
    for a in range(0, 2048, 512):
        v = lax.dot_general(upg, upv[a : a + 512, :], NT, preferred_element_type=F32)
        pb[:, :, :, a : a + 512] = v.reshape(8, 2, 8, 512)
    chain(0, 0, 0)
    chain(0, 1, 0)
    share(0, pb, sxb, rxb)

    for i, (a, w) in enumerate(CUTS):
        got(r1f.at[:, a : a + w], e_r.at[i])
    u = uf[...] + r1f[...].astype(F32)
    uf[...] = u
    hid = (gs[...] * u).astype(BF16)
    for a in range(0, 2048, 512):
        v = lax.dot_general(hid, dnv[:, a : a + 512], NN, preferred_element_type=F32)
        pf[:, :, :, a : a + 512] = v.reshape(8, 2, 8, 512)
    chain(1, 1, 0)
    chain(1, 0, 0)
    share(1, pf, sxf, rxf)

    chain(0, 0, 1)
    chain(0, 1, 1)
    hand(0, pb, rxb, gb, m1b, n1b, sm)
    rows = pl.ds(pl.multiple_of(r * 64, 64), 64)
    gg[...] = (hb[rows, :] * uf[rows, :] * dg[rows, :]).astype(BF16)
    cp_g = fetch(gg, out_g.at[0], 0)
    chain(1, 1, 1)
    chain(1, 0, 1)
    hand(1, pf, rxf, gf, m1f, n1f, sp)
    pl.semaphore_wait(far, 4)
    chain(0, 0, 2)
    chain(0, 1, 2)
    chain(1, 1, 2)
    chain(1, 0, 2)
    chain(0, 0, 3)
    chain(1, 1, 3)

    for t, (n1, land, fr, o, out) in enumerate(((n1b, mb, hb_r, ob, out_b), (n1f, mf, hf_r, of, out_f))):
        got(n1, h1_r.at[t])
        v = n1[...]
        for i in (2, 3, 0, 1):
            got(land.at[i], fr.at[i])
            v = v + land[i].astype(F32)
        o[...] = v.astype(BF16)
        fetch(o, out.at[0], 1 + t)

    for cp in sent:
        cp.wait_send()
    for t in (0, 1):
        for (buf, ss, rs, n), dev in ((plus[t], zp), (minus[t], zm)):
            for d in range(n):
                rc(buf.at[z], buf.at[z], ss.at[d], rs.at[d], dev).wait_send()
    cp_g.wait()
    pltpu.make_async_copy(ob, out_b.at[0], lsem.at[1]).wait()
    pltpu.make_async_copy(of, out_f.at[0], lsem.at[2]).wait()


def writer(a, b, c, x, y, w, av, bv, cv, isem, osem):
    trio = ((a, av, x), (b, bv, y), (c, cv, w))
    loads = [pltpu.make_async_copy(p, v, isem.at[i]) for i, (p, v, _) in enumerate(trio)]
    for cp in loads:
        cp.start()
    stores = [pltpu.make_async_copy(v, q, osem.at[i]) for i, (_, v, q) in enumerate(trio)]
    for i in range(3):
        loads[i].wait()
        stores[i].start()
    for cp in stores:
        cp.wait()


def shards(inputs, gate_pre, up_weight, down_weight, output_grad):
    vm = pltpu.VMEM
    dma = lambda n: [pltpu.SemaphoreType.DMA((n,)), pltpu.SemaphoreType.DMA((n,))]
    blk = lambda *n: vm((*n, 8, 2048), BF16)
    wide = lambda: vm((8, 2048), F32)
    mat = lambda t: vm((128, 896), t)
    any_spec = pl.BlockSpec(memory_space=pl.ANY)
    shapes = (
        jax.ShapeDtypeStruct((1, 8, 2048), BF16),
        jax.ShapeDtypeStruct((1, 64, 896), BF16),
        jax.ShapeDtypeStruct((1, 8, 2048), BF16),
    )
    results = pl.pallas_call(
        kernel,
        out_shape=shapes,
        in_specs=[any_spec] * 5,
        out_specs=(any_spec,) * 3,
        scratch_shapes=[
            blk(8, 2), blk(8, 2), vm((2048, 896), BF16), vm((896, 2048), BF16), mat(BF16), mat(F32), mat(F32),
            mat(F32), mat(F32), mat(BF16), mat(BF16), mat(BF16), mat(BF16), vm((64, 896), BF16),
            vm((8, 2, 8, 2048), F32), vm((8, 2, 8, 2048), F32),
            blk(3, 2), blk(2, 2), blk(4, 2), blk(3, 2), blk(4, 2), blk(3, 2), blk(3, 2), blk(2, 2),
            blk(), blk(), blk(), blk(),
            wide(), wide(), wide(), wide(), blk(4), blk(4), blk(), blk(),
            pltpu.SemaphoreType.DMA((5,)), pltpu.SemaphoreType.REGULAR, pltpu.SemaphoreType.REGULAR,
            *dma(F_LEN[0]), *dma(F_LEN[1]), *dma(B_LEN[0]), *dma(B_LEN[1]), *dma(2),
            *dma(4), *dma(F_LEN[0]), *dma(F_LEN[1]), *dma(B_LEN[0]), *dma(B_LEN[1]), *dma(2),
            *dma(2), *dma(4), *dma(4),
        ],
        compiler_params=pltpu.CompilerParams(
            collective_id=0, has_side_effects=True, vmem_limit_bytes=60 * 1024 * 1024
        ),
        name="ffn",
    )(inputs, gate_pre, up_weight, down_weight, output_grad)
    return pl.pallas_call(
        writer,
        out_shape=shapes,
        in_specs=[any_spec] * 3,
        out_specs=(any_spec,) * 3,
        scratch_shapes=[
            vm((1, 8, 2048), BF16), vm((1, 64, 896), BF16), vm((1, 8, 2048), BF16),
            pltpu.SemaphoreType.DMA((3,)), pltpu.SemaphoreType.DMA((3,)),
        ],
        name="write",
    )(*results)


def solution(mesh):
    placed = (
        P("section", "col", "row"),
        P("section", None, "col"),
        P("row", "col"),
        P("col", "row"),
        P("section", "col", "row"),
    )
    return jax.shard_map(
        shards,
        mesh=mesh,
        in_specs=placed,
        out_specs=(
            P("section", "col", "row"),
            P("section", "row", "col"),
            P("section", "col", "row"),
        ),
        check_vma=False,
    )
```

time: 302 us -> 90 us (0.30)
  the two profiles are of different devices: /device:TPU:60 before, /device:TPU:1 now
where the time goes in v2:
time: 90 us; the launch traced here: 89.9 us
  Pallas kernels  89.2 us (99%)
    pallas_call x1, Pallas kernels, shards(): pl.pallas_call(kernel, out_shape=shapes, in_specs=[any_spec] * 5, out_spe...  87.6 us

profile of v2, /device:TPU:1, one launch (start us, length us, event | category | flops | bytes accessed | tf_op | source)
XLA Modules:
  0.0 89.9 jit_solution(15164138588826375841)
XLA Ops:
  0.6 87.6 %ffn.1 = (bf16[1,8,2048]{2,1,0:T(8,128)(2,1)}, bf16[1,64,896]{2,1,0:T(8,128)(2,1)}, bf16[1,8,2048]{2,1,0:T(8,128)(2,1)}) custom-call(bf16[1,8,2048]{2,1,0:T(8,128)(2,1)} %in_f.1, bf16[1,128,896]{2,1,0:T(8,128)(2,1)} %gate_in.1, bf16[2048,896]{1,0:T(8,128)(2,1)} %up_in.1, bf16[896,2048]{1,0:T(8,128)(2,1)} %dn_in.1, bf16[1,8,2048]{2,1,0:T(8,128)(2,1)} %in_b.1), custom_call_target="tpu_custom_call" | custom-call | tf_op jit(solution)/shard_map/ffn/pallas_call | solution.py:296
  88.2 1.6 %write.1 = (bf16[1,8,2048]{2,1,0:T(8,128)(2,1)}, bf16[1,64,896]{2,1,0:T(8,128)(2,1)}, bf16[1,8,2048]{2,1,0:T(8,128)(2,1)}) custom-call(bf16[1,8,2048]{2,1,0:T(8,128)(2,1)} %get-tuple-element.6.a, bf16[1,64,896]{2,1,0:T(8,128)(2,1)} %get-tuple-element.7.b, bf16[1,8,2048]{2,1,0:T(8,128)(2,1)} %get-tuple-element.8.c), custom_call_target="tpu_custom_call" | custom-call | tf_op jit(solution)/shard_map/write/pallas_call | solution.py:318

commit v3 on v2

v3 whole, which is shorter than its diff:
```python
import jax
import jax.numpy as jnp
from jax import lax
from jax.experimental import pallas as pl
from jax.experimental.pallas import tpu as pltpu
from jax.sharding import PartitionSpec as P

MESH = pl.DeviceIdType.MESH
F32 = jnp.float32
BF16 = jnp.bfloat16
NT = (((1,), (1,)), ((), ()))
NN = (((1,), (0,)), ((), ()))
CUTS = ((0, 512), (512, 384))
B_LEN = (4, 3)
F_LEN = (3, 4)


def kernel(
    in_f, gate_in, up_in, dn_in, in_b,
    out_f, out_g, out_b,
    gf, gb, upv, dnv, gv, gs, dg,
    uf, hb, s1f, r1f, s1b, r1b, gg,
    pf, pb, sfp, rfp, sfm, rfm, sbp, rbp, sbm, rbm, sxf, rxf, sxb, rxb,
    m1f, n1f, m1b, n1b, mf, mb, of, ob,
    lsem, near, far, fzp_s, fzp_r, fzm_s, fzm_r, fx_s, fx_r, bzp_s, bzp_r, bzm_s, bzm_r, bx_s, bx_r,
    e_s, e_r, rfp_s, rfp_r, rfm_s, rfm_r, rbp_s, rbp_r, rbm_s, rbm_r, rx_s, rx_r,
    h1_s, h1_r, hf_s, hf_r, hb_s, hb_r,
):
    s = lax.axis_index("section")
    r = lax.axis_index("row")
    c = lax.axis_index("col")
    z, xl = c // 2, c % 2
    xo = 1 - xl
    ns = lax.axis_size("section")
    sp, sm = (s + 1) % ns, (s + ns - 1) % ns
    up1, dn1 = (z + 1) % 8, (z + 7) % 8
    zp = {"col": up1 * 2 + xl}
    zm = {"col": dn1 * 2 + xl}
    xp = {"col": z * 2 + xo}
    mate = {"row": 1 - r}

    def at(sec, zz, x):
        return {"section": sec, "col": zz * 2 + x}

    def fetch(src, dst, i):
        cp = pltpu.make_async_copy(src, dst, lsem.at[i])
        cp.start()
        return cp

    cp_gate = fetch(gate_in.at[0], gv, 0)
    cp_f = fetch(in_f.at[0], gf.at[z, xl], 1)
    cp_b = fetch(in_b.at[0], gb.at[z, xl], 2)
    cp_dn = fetch(dn_in, dnv, 4)
    cp_up = fetch(up_in, upv, 3)

    barrier = pltpu.get_barrier_semaphore()
    for dev in (zp, zm, xp, mate):
        pl.semaphore_signal(barrier, inc=1, device_id=dev, device_id_type=MESH)

    @pl.when(z == 0)
    def _():
        for sec in (sp, sm):
            pl.semaphore_signal(barrier, inc=1, device_id={"section": sec}, device_id_type=MESH)
        pl.semaphore_wait(barrier, 6)

    @pl.when(z > 0)
    def _():
        pl.semaphore_wait(barrier, 4)

    sent = []

    def rc(src, dst, ss, rs, dev):
        return pltpu.make_async_remote_copy(
            src_ref=src, dst_ref=dst, send_sem=ss, recv_sem=rs, device_id=dev, device_id_type=MESH
        )

    def put(src, dst, ss, rs, dev):
        cp = rc(src, dst, ss, rs, dev)
        cp.start()
        sent.append(cp)

    def got(dst, rs):
        rc(dst, dst, rs, rs, zp).wait_recv()

    put(in_b.at[0], gb.at[z, xl], bx_s.at[0], bx_r.at[0], xp)
    put(in_f.at[0], gf.at[z, xl], fzp_s.at[0], fzp_r.at[0], zp)
    put(in_f.at[0], gf.at[z, xl], fzm_s.at[0], fzm_r.at[0], zm)
    put(in_b.at[0], gb.at[z, xl], bzp_s.at[0], bzp_r.at[0], zp)
    put(in_b.at[0], gb.at[z, xl], bzm_s.at[0], bzm_r.at[0], zm)
    put(in_f.at[0], gf.at[z, xl], fx_s.at[0], fx_r.at[0], xp)

    cp_gate.wait()
    g32 = gv[...].astype(F32)
    sg = 1.0 / (1.0 + jnp.exp(-g32))
    gs[...] = g32 * sg
    dg[...] = sg * (1.0 + g32 * (1.0 - sg))

    got(gb.at[z, xo], bx_r.at[0])
    put(gb.at[z, xo], gb.at[z, xo], bzp_s.at[3], bzp_r.at[3], zp)
    put(gb.at[z, xo], gb.at[z, xo], bzm_s.at[4], bzm_r.at[4], zm)
    for d in range(1, 5):
        lo, hi = (z + 8 - d) % 8, (z + d) % 8
        got(gf.at[lo, xl], fzp_r.at[d - 1])
        if d < 4:
            put(gf.at[lo, xl], gf.at[lo, xl], fzp_s.at[d], fzp_r.at[d], zp)
        put(gf.at[lo, xl], gf.at[lo, xl], fx_s.at[d], fx_r.at[d], xp)
        if d <= 3:
            got(gf.at[hi, xl], fzm_r.at[d - 1])
            if d < 3:
                put(gf.at[hi, xl], gf.at[hi, xl], fzm_s.at[d], fzm_r.at[d], zm)
            put(gf.at[hi, xl], gf.at[hi, xl], fx_s.at[4 + d], fx_r.at[4 + d], xp)
        for half, x in ((0, xl), (1, xo)):
            if d <= 3:
                i = half * 3 + d - 1
                got(gb.at[lo, x], bzp_r.at[i])
                if d < 3:
                    put(gb.at[lo, x], gb.at[lo, x], bzp_s.at[i + 1], bzp_r.at[i + 1], zp)
            i = half * 4 + d - 1
            got(gb.at[hi, x], bzm_r.at[i])
            if d < 4:
                put(gb.at[hi, x], gb.at[hi, x], bzm_s.at[i + 1], bzm_r.at[i + 1], zm)
    got(gf.at[z, xo], fx_r.at[0])
    for d in range(1, 5):
        got(gf.at[(z + 8 - d) % 8, xo], fx_r.at[d])
        if d <= 3:
            got(gf.at[(z + d) % 8, xo], fx_r.at[4 + d])
    cp_f.wait()
    cp_b.wait()

    @pl.when(z == 0)
    def _():
        for sec in (sp, sm):
            pl.semaphore_signal(far, inc=1, device_id={"section": sec}, device_id_type=MESH)

    cp_up.wait()
    act = gf[...].reshape(128, 2048)
    for i, (a, w) in enumerate(CUTS):
        v = lax.dot_general(act, upv[:, a : a + w], NN, preferred_element_type=F32)
        uf[:, a : a + w] = v
        s1f[:, a : a + w] = v.astype(BF16)
        put(s1f.at[:, a : a + w], r1f.at[:, a : a + w], e_s.at[i], e_r.at[i], mate)

    cp_dn.wait()
    grd = gb[...].reshape(128, 2048)
    for i, (a, w) in enumerate(CUTS):
        v = lax.dot_general(grd, dnv[a : a + w, :], NT, preferred_element_type=F32)
        hb[:, a : a + w] = v
        s1b[:, a : a + w] = v.astype(BF16)
        put(s1b.at[:, a : a + w], r1b.at[:, a : a + w], e_s.at[2 + i], e_r.at[2 + i], mate)

    chains = {
        (0, 0): (pb, sbp, rbp, rbp_s, rbp_r, B_LEN[0]),
        (0, 1): (pb, sbm, rbm, rbm_s, rbm_r, B_LEN[1]),
        (1, 0): (pf, sfp, rfp, rfp_s, rfp_r, F_LEN[0]),
        (1, 1): (pf, sfm, rfm, rfm_s, rfm_r, F_LEN[1]),
    }
    ends = {0: (mb, hb_s, hb_r, sm), 1: (mf, hf_s, hf_r, sp)}

    def chain(t, way, k):
        part, snd, rcv, ss, rs, n = chains[t, way]
        if k >= n:
            return
        d = n - k
        target = (z + d) % 8 if way == 0 else (z + 8 - d) % 8
        for j, x in enumerate((xl, xo)):
            v = part[target, x]
            if k > 0:
                got(rcv.at[k - 1, x], rs.at[2 * k - 2 + j])
                v = v + rcv[k - 1, x].astype(F32)
            snd[k, x] = v.astype(BF16)
            if d > 1:
                put(snd.at[k, x], rcv.at[k, x], ss.at[2 * k + j], rs.at[2 * k + j], zp if way == 0 else zm)
            else:
                land, fs, fr, sec = ends[t]
                i = way * 2 + j
                put(snd.at[k, x], land.at[i], fs.at[i], fr.at[i], at(sec, target, x))

    def share(t, part, snd, rcv):
        snd[...] = part[z, xo].astype(BF16)
        put(snd, rcv, rx_s.at[t], rx_r.at[t], xp)

    def hand(t, part, rcv, buf, m, n, sec):
        got(rcv, rx_r.at[t])
        m[...] = part[z, xl] + buf[z, xl].astype(F32) + rcv[...].astype(F32)
        put(m, n, h1_s.at[t], h1_r.at[t], at(sec, z, xl))

    for i, (a, w) in enumerate(CUTS):
        got(r1f.at[:, a : a + w], e_r.at[i])
    u = uf[...] + r1f[...].astype(F32)
    uf[...] = u
    hid = (gs[...] * u).astype(BF16)
    for a in range(0, 2048, 512):
        v = lax.dot_general(hid, dnv[:, a : a + 512], NN, preferred_element_type=F32)
        pf[:, :, :, a : a + 512] = v.reshape(8, 2, 8, 512)
    share(1, pf, sxf, rxf)
    chain(1, 1, 0)
    chain(1, 0, 0)

    for i, (a, w) in enumerate(CUTS):
        got(r1b.at[:, a : a + w], e_r.at[2 + i])
    h = hb[...] + r1b[...].astype(F32)
    hb[...] = h
    upg = (gs[...] * h).astype(BF16)
    for a in range(0, 2048, 512):
        v = lax.dot_general(upg, upv[a : a + 512, :], NT, preferred_element_type=F32)
        pb[:, :, :, a : a + 512] = v.reshape(8, 2, 8, 512)
    share(0, pb, sxb, rxb)
    chain(0, 0, 0)
    chain(0, 1, 0)

    chain(1, 1, 1)
    chain(1, 0, 1)

    @pl.when(z == 0)
    def _():
        pl.semaphore_wait(far, 2)
        for k in range(1, 8):
            pl.semaphore_signal(near, inc=1, device_id={"col": k * 2 + xl}, device_id_type=MESH)

    rows = pl.ds(pl.multiple_of(r * 64, 64), 64)
    gg[...] = (hb[rows, :] * uf[rows, :] * dg[rows, :]).astype(BF16)
    cp_g = fetch(gg, out_g.at[0], 0)
    chain(0, 0, 1)
    chain(0, 1, 1)

    @pl.when(z > 0)
    def _():
        pl.semaphore_wait(near, 1)

    chain(1, 1, 2)
    chain(1, 0, 2)
    hand(1, pf, rxf, gf, m1f, n1f, sp)
    chain(0, 0, 2)
    chain(0, 1, 2)
    hand(0, pb, rxb, gb, m1b, n1b, sm)
    chain(1, 1, 3)
    chain(0, 0, 3)

    for t, (n1, land, fr, o, out) in ((1, (n1f, mf, hf_r, of, out_f)), (0, (n1b, mb, hb_r, ob, out_b))):
        got(n1, h1_r.at[t])
        v = n1[...]
        for i in (2, 3, 0, 1):
            got(land.at[i], fr.at[i])
            v = v + land[i].astype(F32)
        o[...] = v.astype(BF16)
        fetch(o, out.at[0], 1 + t)

    for cp in sent:
        cp.wait_send()
    cp_g.wait()
    pltpu.make_async_copy(ob, out_b.at[0], lsem.at[1]).wait()
    pltpu.make_async_copy(of, out_f.at[0], lsem.at[2]).wait()


def writer(a, b, c, x, y, w, av, bv, cv, isem, osem):
    trio = ((a, av, x), (b, bv, y), (c, cv, w))
    loads = [pltpu.make_async_copy(p, v, isem.at[i]) for i, (p, v, _) in enumerate(trio)]
    for cp in loads:
        cp.start()
    stores = [pltpu.make_async_copy(v, q, osem.at[i]) for i, (_, v, q) in enumerate(trio)]
    for i in range(3):
        loads[i].wait()
        stores[i].start()
    for cp in stores:
        cp.wait()


def shards(inputs, gate_pre, up_weight, down_weight, output_grad):
    vm = pltpu.VMEM
    dma = lambda n: [pltpu.SemaphoreType.DMA((n,)), pltpu.SemaphoreType.DMA((n,))]
    blk = lambda *n: vm((*n, 8, 2048), BF16)
    wide = lambda: vm((8, 2048), F32)
    mat = lambda t: vm((128, 896), t)
    any_spec = pl.BlockSpec(memory_space=pl.ANY)
    shapes = (
        jax.ShapeDtypeStruct((1, 8, 2048), BF16),
        jax.ShapeDtypeStruct((1, 64, 896), BF16),
        jax.ShapeDtypeStruct((1, 8, 2048), BF16),
    )
    results = pl.pallas_call(
        kernel,
        out_shape=shapes,
        in_specs=[any_spec] * 5,
        out_specs=(any_spec,) * 3,
        scratch_shapes=[
            blk(8, 2), blk(8, 2), vm((2048, 896), BF16), vm((896, 2048), BF16), mat(BF16), mat(F32), mat(F32),
            mat(F32), mat(F32), mat(BF16), mat(BF16), mat(BF16), mat(BF16), vm((64, 896), BF16),
            vm((8, 2, 8, 2048), F32), vm((8, 2, 8, 2048), F32),
            blk(3, 2), blk(2, 2), blk(4, 2), blk(3, 2), blk(4, 2), blk(3, 2), blk(3, 2), blk(2, 2),
            blk(), blk(), blk(), blk(),
            wide(), wide(), wide(), wide(), blk(4), blk(4), blk(), blk(),
            pltpu.SemaphoreType.DMA((5,)), pltpu.SemaphoreType.REGULAR, pltpu.SemaphoreType.REGULAR,
            *dma(4), *dma(3), *dma(8), *dma(6), *dma(8), *dma(1),
            *dma(4), *dma(2 * F_LEN[0]), *dma(2 * F_LEN[1]), *dma(2 * B_LEN[0]), *dma(2 * B_LEN[1]), *dma(2),
            *dma(2), *dma(4), *dma(4),
        ],
        compiler_params=pltpu.CompilerParams(
            collective_id=0, has_side_effects=True, vmem_limit_bytes=60 * 1024 * 1024
        ),
        name="ffn",
    )(inputs, gate_pre, up_weight, down_weight, output_grad)
    return pl.pallas_call(
        writer,
        out_shape=shapes,
        in_specs=[any_spec] * 3,
        out_specs=(any_spec,) * 3,
        scratch_shapes=[
            vm((1, 8, 2048), BF16), vm((1, 64, 896), BF16), vm((1, 8, 2048), BF16),
            pltpu.SemaphoreType.DMA((3,)), pltpu.SemaphoreType.DMA((3,)),
        ],
        name="write",
    )(*results)


def solution(mesh):
    placed = (
        P("section", "col", "row"),
        P("section", None, "col"),
        P("row", "col"),
        P("col", "row"),
        P("section", "col", "row"),
    )
    return jax.shard_map(
        shards,
        mesh=mesh,
        in_specs=placed,
        out_specs=(
            P("section", "col", "row"),
            P("section", "row", "col"),
            P("section", "col", "row"),
        ),
        check_vma=False,
    )
```

time: 90 us -> 63 us (0.70)
  Pallas kernels: 89.2 us -> 62.2 us
    pallas_call x1, Pallas kernels: 87.6 us -> 60.6 us  [shards(): pl.pallas_call(kernel, out_shape=shapes, in_specs=[any_spec] * 5, out_spe...]
where the time goes in v3:
time: 63 us; the launch traced here: 62.8 us
  Pallas kernels  62.2 us (99%)
  between operations  0.64 us (1%)
    pallas_call x1, Pallas kernels, shards(): pl.pallas_call(kernel, out_shape=shapes, in_specs=[any_spec] * 5, out_spe...  60.6 us
    pallas_call x1, Pallas kernels, shards(): pl.pallas_call(writer, out_shape=shapes, in_specs=[any_spec] * 3, out_spe...  1.62 us

profile of v3, /device:TPU:1, one launch (start us, length us, event | category | flops | bytes accessed | tf_op | source)
XLA Modules:
  0.0 62.8 jit_solution(15640241869763433260)
XLA Ops:
  0.6 60.6 %ffn.1 = (bf16[1,8,2048]{2,1,0:T(8,128)(2,1)}, bf16[1,64,896]{2,1,0:T(8,128)(2,1)}, bf16[1,8,2048]{2,1,0:T(8,128)(2,1)}) custom-call(bf16[1,8,2048]{2,1,0:T(8,128)(2,1)} %in_f.1, bf16[1,128,896]{2,1,0:T(8,128)(2,1)} %gate_in.1, bf16[2048,896]{1,0:T(8,128)(2,1)} %up_in.1, bf16[896,2048]{1,0:T(8,128)(2,1)} %dn_in.1, bf16[1,8,2048]{2,1,0:T(8,128)(2,1)} %in_b.1), custom_call_target="tpu_custom_call" | custom-call | tf_op jit(solution)/shard_map/ffn/pallas_call | solution.py:280
  61.2 1.6 %write.1 = (bf16[1,8,2048]{2,1,0:T(8,128)(2,1)}, bf16[1,64,896]{2,1,0:T(8,128)(2,1)}, bf16[1,8,2048]{2,1,0:T(8,128)(2,1)}) custom-call(bf16[1,8,2048]{2,1,0:T(8,128)(2,1)} %get-tuple-element.6.a, bf16[1,64,896]{2,1,0:T(8,128)(2,1)} %get-tuple-element.7.b, bf16[1,8,2048]{2,1,0:T(8,128)(2,1)} %get-tuple-element.8.c), custom_call_target="tpu_custom_call" | custom-call | tf_op jit(solution)/shard_map/write/pallas_call | solution.py:302

commit v4 on v3

--- a/solution.py
+++ b/solution.py
@@ -19,9 +19,9 @@
     in_f, gate_in, up_in, dn_in, in_b,
     out_f, out_g, out_b,
     gf, gb, upv, dnv, gv, gs, dg,
-    uf, hb, s1f, r1f, s1b, r1b, gg,
+    uf, hb, s1f, r1f, s1b, r1b,
     pf, pb, sfp, rfp, sfm, rfm, sbp, rbp, sbm, rbm, sxf, rxf, sxb, rxb,
-    m1f, n1f, m1b, n1b, mf, mb, of, ob,
+    m1f, n1f, m1b, n1b, mf, mb,
     lsem, near, far, fzp_s, fzp_r, fzm_s, fzm_r, fx_s, fx_r, bzp_s, bzp_r, bzm_s, bzm_r, bx_s, bx_r,
     e_s, e_r, rfp_s, rfp_r, rfm_s, rfm_r, rbp_s, rbp_r, rbm_s, rbm_r, rx_s, rx_r,
     h1_s, h1_r, hf_s, hf_r, hb_s, hb_r,
@@ -218,8 +218,7 @@
             pl.semaphore_signal(near, inc=1, device_id={"col": k * 2 + xl}, device_id_type=MESH)
 
     rows = pl.ds(pl.multiple_of(r * 64, 64), 64)
-    gg[...] = (hb[rows, :] * uf[rows, :] * dg[rows, :]).astype(BF16)
-    cp_g = fetch(gg, out_g.at[0], 0)
+    out_g[0] = (hb[rows, :] * uf[rows, :] * dg[rows, :]).astype(BF16)
     chain(0, 0, 1)
     chain(0, 1, 1)
 
@@ -236,31 +235,22 @@
     chain(1, 1, 3)
     chain(0, 0, 3)
 
-    for t, (n1, land, fr, o, out) in ((1, (n1f, mf, hf_r, of, out_f)), (0, (n1b, mb, hb_r, ob, out_b))):
+    for t, (n1, land, fr, out) in ((1, (n1f, mf, hf_r, out_f)), (0, (n1b, mb, hb_r, out_b))):
         got(n1, h1_r.at[t])
         v = n1[...]
         for i in (2, 3, 0, 1):
             got(land.at[i], fr.at[i])
             v = v + land[i].astype(F32)
-        o[...] = v.astype(BF16)
-        fetch(o, out.at[0], 1 + t)
+        out[0] = v.astype(BF16)
 
     for cp in sent:
         cp.wait_send()
-    cp_g.wait()
-    pltpu.make_async_copy(ob, out_b.at[0], lsem.at[1]).wait()
-    pltpu.make_async_copy(of, out_f.at[0], lsem.at[2]).wait()
-
-
-def writer(a, b, c, x, y, w, av, bv, cv, isem, osem):
-    trio = ((a, av, x), (b, bv, y), (c, cv, w))
-    loads = [pltpu.make_async_copy(p, v, isem.at[i]) for i, (p, v, _) in enumerate(trio)]
-    for cp in loads:
+
+
+def writer(a, b, c, x, y, w, sem):
+    stores = [pltpu.make_async_copy(p, q, sem.at[i]) for i, (p, q) in enumerate(((a, x), (b, y), (c, w)))]
+    for cp in stores:
         cp.start()
-    stores = [pltpu.make_async_copy(v, q, osem.at[i]) for i, (_, v, q) in enumerate(trio)]
-    for i in range(3):
-        loads[i].wait()
-        stores[i].start()
     for cp in stores:
         cp.wait()
 
@@ -272,6 +262,7 @@
     wide = lambda: vm((8, 2048), F32)
     mat = lambda t: vm((128, 896), t)
     any_spec = pl.BlockSpec(memory_space=pl.ANY)
+    in_vmem = pl.BlockSpec(memory_space=pltpu.VMEM)
     shapes = (
         jax.ShapeDtypeStruct((1, 8, 2048), BF16),
         jax.ShapeDtypeStruct((1, 64, 896), BF16),
@@ -279,16 +270,16 @@
     )
     results = pl.pallas_call(
         kernel,
-        out_shape=shapes,
+        out_shape=tuple(vm(x.shape, x.dtype) for x in shapes),
         in_specs=[any_spec] * 5,
-        out_specs=(any_spec,) * 3,
+        out_specs=(in_vmem,) * 3,
         scratch_shapes=[
             blk(8, 2), blk(8, 2), vm((2048, 896), BF16), vm((896, 2048), BF16), mat(BF16), mat(F32), mat(F32),
-            mat(F32), mat(F32), mat(BF16), mat(BF16), mat(BF16), mat(BF16), vm((64, 896), BF16),
+            mat(F32), mat(F32), mat(BF16), mat(BF16), mat(BF16), mat(BF16),
             vm((8, 2, 8, 2048), F32), vm((8, 2, 8, 2048), F32),
             blk(3, 2), blk(2, 2), blk(4, 2), blk(3, 2), blk(4, 2), blk(3, 2), blk(3, 2), blk(2, 2),
             blk(), blk(), blk(), blk(),
-            wide(), wide(), wide(), wide(), blk(4), blk(4), blk(), blk(),
+            wide(), wide(), wide(), wide(), blk(4), blk(4),
             pltpu.SemaphoreType.DMA((5,)), pltpu.SemaphoreType.REGULAR, pltpu.SemaphoreType.REGULAR,
             *dma(4), *dma(3), *dma(8), *dma(6), *dma(8), *dma(1),
             *dma(4), *dma(2 * F_LEN[0]), *dma(2 * F_LEN[1]), *dma(2 * B_LEN[0]), *dma(2 * B_LEN[1]), *dma(2),
@@ -302,14 +293,11 @@
     return pl.pallas_call(
         writer,
         out_shape=shapes,
-        in_specs=[any_spec] * 3,
+        in_specs=[in_vmem] * 3,
         out_specs=(any_spec,) * 3,
-        scratch_shapes=[
-            vm((1, 8, 2048), BF16), vm((1, 64, 896), BF16), vm((1, 8, 2048), BF16),
-            pltpu.SemaphoreType.DMA((3,)), pltpu.SemaphoreType.DMA((3,)),
-        ],
+        scratch_shapes=[pltpu.SemaphoreType.DMA((3,))],
         name="write",
-    )(*results)
+    )(*(pltpu.with_memory_space_constraint(x, pltpu.VMEM) for x in results))
 
 
 def solution(mesh):

time: 63 us -> 61.5 us (0.976)
  Pallas kernels: 62.2 us -> 60.8 us
    pallas_call x2, Pallas kernels: 62.2 us -> 60.8 us  [the longest x1 60.1 us: shards(): pl.pallas_call(kernel, out_shape=tuple((vm(x.shape, x.dtype) for x in sha...]
where the time goes in v4:
time: 61.5 us; the launch traced here: 61.4 us
  Pallas kernels  60.8 us (99%)
  between operations  0.64 us (1%)
    pallas_call x1, Pallas kernels, shards(): pl.pallas_call(kernel, out_shape=tuple((vm(x.shape, x.dtype) for x in sha...  60.1 us

profile of v4, /device:TPU:1, one launch (start us, length us, event | category | flops | bytes accessed | tf_op | source)
XLA Modules:
  0.0 61.4 jit_solution(955995461057783872)
XLA Ops:
  0.6 60.1 %ffn.1 = (bf16[1,8,2048]{2,1,0:T(8,128)(2,1)S(1)}, bf16[1,64,896]{2,1,0:T(8,128)(2,1)S(1)}, bf16[1,8,2048]{2,1,0:T(8,128)(2,1)S(1)}) custom-call(bf16[1,8,2048]{2,1,0:T(8,128)(2,1)} %in_f.1, bf16[1,128,896]{2,1,0:T(8,128)(2,1)} %gate_in.1, bf16[2048,896]{1,0:T(8,128)(2,1)} %up_in.1, bf16[896,2048]{1,0:T(8,128)(2,1)} %dn_in.1, bf16[1,8,2048]{2,1,0:T(8,128)(2,1)} %in_b.1), custom_call_target="tpu_custom_call" | custom-call | tf_op jit(solution)/shard_map/ffn/pallas_call | solution.py:271
  60.7 0.7 %write.1 = (bf16[1,8,2048]{2,1,0:T(8,128)(2,1)}, bf16[1,64,896]{2,1,0:T(8,128)(2,1)}, bf16[1,8,2048]{2,1,0:T(8,128)(2,1)}) custom-call(bf16[1,8,2048]{2,1,0:T(8,128)(2,1)S(1)} %get-tuple-element.6.a, bf16[1,64,896]{2,1,0:T(8,128)(2,1)S(1)} %get-tuple-element.7.b, bf16[1,8,2048]{2,1,0:T(8,128)(2,1)S(1)} %get-tuple-element.8.c), custom_call_target="tpu_custom_call" | custom-call | tf_op jit(solution)/shard_map/write/pallas_call | solution.py:293

commit v5 on v4

--- a/solution.py
+++ b/solution.py
@@ -38,6 +38,8 @@
     zm = {"col": dn1 * 2 + xl}
     xp = {"col": z * 2 + xo}
     mate = {"row": 1 - r}
+    zp2 = {"col": ((z + 2) % 8) * 2 + xl}
+    zm2 = {"col": ((z + 6) % 8) * 2 + xl}
 
     def at(sec, zz, x):
         return {"section": sec, "col": zz * 2 + x}
@@ -101,8 +103,10 @@
     for d in range(1, 5):
         lo, hi = (z + 8 - d) % 8, (z + d) % 8
         got(gf.at[lo, xl], fzp_r.at[d - 1])
-        if d < 4:
+        if d < 3:
             put(gf.at[lo, xl], gf.at[lo, xl], fzp_s.at[d], fzp_r.at[d], zp)
+        if d == 2:
+            put(gf.at[lo, xl], gf.at[lo, xl], fzp_s.at[3], fzp_r.at[3], zp2)
         put(gf.at[lo, xl], gf.at[lo, xl], fx_s.at[d], fx_r.at[d], xp)
         if d <= 3:
             got(gf.at[hi, xl], fzm_r.at[d - 1])
@@ -117,15 +121,25 @@
                     put(gb.at[lo, x], gb.at[lo, x], bzp_s.at[i + 1], bzp_r.at[i + 1], zp)
             i = half * 4 + d - 1
             got(gb.at[hi, x], bzm_r.at[i])
-            if d < 4:
+            if d < 3:
                 put(gb.at[hi, x], gb.at[hi, x], bzm_s.at[i + 1], bzm_r.at[i + 1], zm)
+            if d == 2:
+                put(gb.at[hi, x], gb.at[hi, x], bzm_s.at[i + 2], bzm_r.at[i + 2], zm2)
+    cp_b.wait()
+    cp_dn.wait()
+    grd = gb[...].reshape(128, 2048)
+    for i, (a, w) in enumerate(CUTS):
+        v = lax.dot_general(grd, dnv[a : a + w, :], NT, preferred_element_type=F32)
+        hb[:, a : a + w] = v
+        s1b[:, a : a + w] = v.astype(BF16)
+        put(s1b.at[:, a : a + w], r1b.at[:, a : a + w], e_s.at[2 + i], e_r.at[2 + i], mate)
+
     got(gf.at[z, xo], fx_r.at[0])
     for d in range(1, 5):
         got(gf.at[(z + 8 - d) % 8, xo], fx_r.at[d])
         if d <= 3:
             got(gf.at[(z + d) % 8, xo], fx_r.at[4 + d])
     cp_f.wait()
-    cp_b.wait()
 
     @pl.when(z == 0)
     def _():
@@ -139,14 +153,6 @@
         uf[:, a : a + w] = v
         s1f[:, a : a + w] = v.astype(BF16)
         put(s1f.at[:, a : a + w], r1f.at[:, a : a + w], e_s.at[i], e_r.at[i], mate)
-
-    cp_dn.wait()
-    grd = gb[...].reshape(128, 2048)
-    for i, (a, w) in enumerate(CUTS):
-        v = lax.dot_general(grd, dnv[a : a + w, :], NT, preferred_element_type=F32)
-        hb[:, a : a + w] = v
-        s1b[:, a : a + w] = v.astype(BF16)
-        put(s1b.at[:, a : a + w], r1b.at[:, a : a + w], e_s.at[2 + i], e_r.at[2 + i], mate)
 
     chains = {
         (0, 0): (pb, sbp, rbp, rbp_s, rbp_r, B_LEN[0]),
@@ -185,6 +191,18 @@
         put(m, n, h1_s.at[t], h1_r.at[t], at(sec, z, xl))
 
     for i, (a, w) in enumerate(CUTS):
+        got(r1b.at[:, a : a + w], e_r.at[2 + i])
+    h = hb[...] + r1b[...].astype(F32)
+    hb[...] = h
+    upg = (gs[...] * h).astype(BF16)
+    for a in range(0, 2048, 512):
+        v = lax.dot_general(upg, upv[a : a + 512, :], NT, preferred_element_type=F32)
+        pb[:, :, :, a : a + 512] = v.reshape(8, 2, 8, 512)
+    share(0, pb, sxb, rxb)
+    chain(0, 0, 0)
+    chain(0, 1, 0)
+
+    for i, (a, w) in enumerate(CUTS):
         got(r1f.at[:, a : a + w], e_r.at[i])
     u = uf[...] + r1f[...].astype(F32)
     uf[...] = u
@@ -196,20 +214,8 @@
     chain(1, 1, 0)
     chain(1, 0, 0)
 
-    for i, (a, w) in enumerate(CUTS):
-        got(r1b.at[:, a : a + w], e_r.at[2 + i])
-    h = hb[...] + r1b[...].astype(F32)
-    hb[...] = h
-    upg = (gs[...] * h).astype(BF16)
-    for a in range(0, 2048, 512):
-        v = lax.dot_general(upg, upv[a : a + 512, :], NT, preferred_element_type=F32)
-        pb[:, :, :, a : a + 512] = v.reshape(8, 2, 8, 512)
-    share(0, pb, sxb, rxb)
-    chain(0, 0, 0)
-    chain(0, 1, 0)
-
-    chain(1, 1, 1)
-    chain(1, 0, 1)
+    chain(0, 0, 1)
+    chain(0, 1, 1)
 
     @pl.when(z == 0)
     def _():
@@ -219,23 +225,23 @@
 
     rows = pl.ds(pl.multiple_of(r * 64, 64), 64)
     out_g[0] = (hb[rows, :] * uf[rows, :] * dg[rows, :]).astype(BF16)
-    chain(0, 0, 1)
-    chain(0, 1, 1)
+    chain(1, 1, 1)
+    chain(1, 0, 1)
 
     @pl.when(z > 0)
     def _():
         pl.semaphore_wait(near, 1)
 
+    chain(0, 0, 2)
+    chain(0, 1, 2)
+    hand(0, pb, rxb, gb, m1b, n1b, sm)
     chain(1, 1, 2)
     chain(1, 0, 2)
     hand(1, pf, rxf, gf, m1f, n1f, sp)
-    chain(0, 0, 2)
-    chain(0, 1, 2)
-    hand(0, pb, rxb, gb, m1b, n1b, sm)
+    chain(0, 0, 3)
     chain(1, 1, 3)
-    chain(0, 0, 3)
-
-    for t, (n1, land, fr, out) in ((1, (n1f, mf, hf_r, out_f)), (0, (n1b, mb, hb_r, out_b))):
+
+    for t, (n1, land, fr, out) in ((0, (n1b, mb, hb_r, out_b)), (1, (n1f, mf, hf_r, out_f))):
         got(n1, h1_r.at[t])
         v = n1[...]
         for i in (2, 3, 0, 1):

time: 61.5 us -> 61.2 us (level)
  the two profiles are of different devices: /device:TPU:1 before, /device:TPU:2 now
where the time goes in v5:
time: 61.2 us; the launch traced here: 61.1 us
  Pallas kernels  60.5 us (99%)
  between operations  0.64 us (1%)
    pallas_call x1, Pallas kernels, shards(): pl.pallas_call(kernel, out_shape=tuple((vm(x.shape, x.dtype) for x in sha...  59.8 us

profile of v5, /device:TPU:2, one launch (start us, length us, event | category | flops | bytes accessed | tf_op | source)
XLA Modules:
  0.0 61.1 jit_solution(6376577684736564828)
XLA Ops:
  0.6 59.8 %ffn.1 = (bf16[1,8,2048]{2,1,0:T(8,128)(2,1)S(1)}, bf16[1,64,896]{2,1,0:T(8,128)(2,1)S(1)}, bf16[1,8,2048]{2,1,0:T(8,128)(2,1)S(1)}) custom-call(bf16[1,8,2048]{2,1,0:T(8,128)(2,1)} %in_f.1, bf16[1,128,896]{2,1,0:T(8,128)(2,1)} %gate_in.1, bf16[2048,896]{1,0:T(8,128)(2,1)} %up_in.1, bf16[896,2048]{1,0:T(8,128)(2,1)} %dn_in.1, bf16[1,8,2048]{2,1,0:T(8,128)(2,1)} %in_b.1), custom_call_target="tpu_custom_call" | custom-call | tf_op jit(solution)/shard_map/ffn/pallas_call | solution.py:277
  60.4 0.7 %write.1 = (bf16[1,8,2048]{2,1,0:T(8,128)(2,1)}, bf16[1,64,896]{2,1,0:T(8,128)(2,1)}, bf16[1,8,2048]{2,1,0:T(8,128)(2,1)}) custom-call(bf16[1,8,2048]{2,1,0:T(8,128)(2,1)S(1)} %get-tuple-element.6.a, bf16[1,64,896]{2,1,0:T(8,128)(2,1)S(1)} %get-tuple-element.7.b, bf16[1,8,2048]{2,1,0:T(8,128)(2,1)S(1)} %get-tuple-element.8.c), custom_call_target="tpu_custom_call" | custom-call | tf_op jit(solution)/shard_map/write/pallas_call | solution.py:299

commit v6 on v5

--- a/solution.py
+++ b/solution.py
@@ -12,7 +12,7 @@
 NN = (((1,), (0,)), ((), ()))
 CUTS = ((0, 512), (512, 384))
 B_LEN = (4, 3)
-F_LEN = (3, 4)
+F_LEN = (4, 3)
 
 
 def kernel(
@@ -211,8 +211,8 @@
         v = lax.dot_general(hid, dnv[:, a : a + 512], NN, preferred_element_type=F32)
         pf[:, :, :, a : a + 512] = v.reshape(8, 2, 8, 512)
     share(1, pf, sxf, rxf)
+    chain(1, 0, 0)
     chain(1, 1, 0)
-    chain(1, 0, 0)
 
     chain(0, 0, 1)
     chain(0, 1, 1)
@@ -225,8 +225,8 @@
 
     rows = pl.ds(pl.multiple_of(r * 64, 64), 64)
     out_g[0] = (hb[rows, :] * uf[rows, :] * dg[rows, :]).astype(BF16)
+    chain(1, 0, 1)
     chain(1, 1, 1)
-    chain(1, 0, 1)
 
     @pl.when(z > 0)
     def _():
@@ -235,11 +235,11 @@
     chain(0, 0, 2)
     chain(0, 1, 2)
     hand(0, pb, rxb, gb, m1b, n1b, sm)
+    chain(1, 0, 2)
     chain(1, 1, 2)
-    chain(1, 0, 2)
     hand(1, pf, rxf, gf, m1f, n1f, sp)
     chain(0, 0, 3)
-    chain(1, 1, 3)
+    chain(1, 0, 3)
 
     for t, (n1, land, fr, out) in ((0, (n1b, mb, hb_r, out_b)), (1, (n1f, mf, hf_r, out_f))):
         got(n1, h1_r.at[t])
@@ -283,7 +283,7 @@
             blk(8, 2), blk(8, 2), vm((2048, 896), BF16), vm((896, 2048), BF16), mat(BF16), mat(F32), mat(F32),
             mat(F32), mat(F32), mat(BF16), mat(BF16), mat(BF16), mat(BF16),
             vm((8, 2, 8, 2048), F32), vm((8, 2, 8, 2048), F32),
-            blk(3, 2), blk(2, 2), blk(4, 2), blk(3, 2), blk(4, 2), blk(3, 2), blk(3, 2), blk(2, 2),
+            blk(4, 2), blk(3, 2), blk(3, 2), blk(2, 2), blk(4, 2), blk(3, 2), blk(3, 2), blk(2, 2),
             blk(), blk(), blk(), blk(),
             wide(), wide(), wide(), wide(), blk(4), blk(4),
             pltpu.SemaphoreType.DMA((5,)), pltpu.SemaphoreType.REGULAR, pltpu.SemaphoreType.REGULAR,

time: 61.2 us -> 63.1 us (1.031)
  Pallas kernels: 60.5 us -> 62.3 us
    pallas_call x1, Pallas kernels: 59.8 us -> 61.6 us  [shards(): pl.pallas_call(kernel, out_shape=tuple((vm(x.shape, x.dtype) for x in sha...]
where the time goes in v6:
time: 63.1 us; the launch traced here: 62.9 us
  Pallas kernels  62.3 us (99%)
  between operations  0.64 us (1%)
    pallas_call x1, Pallas kernels, shards(): pl.pallas_call(kernel, out_shape=tuple((vm(x.shape, x.dtype) for x in sha...  61.6 us

profile of v6, /device:TPU:2, one launch (start us, length us, event | category | flops | bytes accessed | tf_op | source)
XLA Modules:
  0.0 62.9 jit_solution(2498651692830800458)
XLA Ops:
  0.6 61.6 %ffn.1 = (bf16[1,8,2048]{2,1,0:T(8,128)(2,1)S(1)}, bf16[1,64,896]{2,1,0:T(8,128)(2,1)S(1)}, bf16[1,8,2048]{2,1,0:T(8,128)(2,1)S(1)}) custom-call(bf16[1,8,2048]{2,1,0:T(8,128)(2,1)} %in_f.1, bf16[1,128,896]{2,1,0:T(8,128)(2,1)} %gate_in.1, bf16[2048,896]{1,0:T(8,128)(2,1)} %up_in.1, bf16[896,2048]{1,0:T(8,128)(2,1)} %dn_in.1, bf16[1,8,2048]{2,1,0:T(8,128)(2,1)} %in_b.1), custom_call_target="tpu_custom_call" | custom-call | tf_op jit(solution)/shard_map/ffn/pallas_call | solution.py:277
  62.2 0.7 %write.1 = (bf16[1,8,2048]{2,1,0:T(8,128)(2,1)}, bf16[1,64,896]{2,1,0:T(8,128)(2,1)}, bf16[1,8,2048]{2,1,0:T(8,128)(2,1)}) custom-call(bf16[1,8,2048]{2,1,0:T(8,128)(2,1)S(1)} %get-tuple-element.6.a, bf16[1,64,896]{2,1,0:T(8,128)(2,1)S(1)} %get-tuple-element.7.b, bf16[1,8,2048]{2,1,0:T(8,128)(2,1)S(1)} %get-tuple-element.8.c), custom_call_target="tpu_custom_call" | custom-call | tf_op jit(solution)/shard_map/write/pallas_call | solution.py:299
